TPU v7x, 32 devices: a whole 2x2x4 slice. The times are simulated.
32 devices in a mesh: blk: 8 (over z, core), col: 4 (over y, x).
Axes of the slice: x: 2, y: 2, z: 4, core: 2. Of those that a mesh axis runs over, the one named last changes fastest.
Arguments:
- stiffness: bfloat16 [64, 3, 128, 128], P('blk'), may hold values from -0.3125 to 0.3125
- block_cols: int32 [64, 3], P('blk'), may hold values from 0 to 63, as said below
- basis: bfloat16 [8192, 3, 512], P('blk', None, 'col'), may hold values from -1.1953125 to 1.1953125
- patch_reach: int32 [8, 512, 2], P(None, 'col'), may hold values from 0 to 8
Outputs:
- coarse: float32 [4096, 5, 512], P(('blk', 'col'))
Inputs may be any that keep to these rules, and one draw needn't show every extreme that they name: `block_cols`: block row b lists block row b first and then two other distinct block rows among b - 2 .. b + 2 (periodic); the first block row of each slab lists b - 2 and b + 2.
All inputs are finite; a program needn't handle non-finite values.
Results may differ from a plain program's by a relative error of at most 0.0029.
Values may be sent and summed in bfloat16 or wider, within the bound.
No kernel may reach another device: no remote copies, remote signals or barrier semaphores. Data moves between devices by JAX's collectives and lax.ppermute only.
A program may use at most 64 MiB of HBM per device.

v0:
```python
import jax
import jax.numpy as jnp
from jax import lax
from jax.sharding import PartitionSpec as P


def extended_2(array, sides, width):
    for axis, dim in sides:
        peers, length = (lax.axis_size(axis), array.shape[dim])
        up = [(i, (i + 1) % peers) for i in range(peers)]
        down = [(j, i) for i, j in up]
        last = lax.slice_in_dim(array, length - width, length, axis=dim)
        leading = lax.slice_in_dim(array, 0, width, axis=dim)
        before = lax.ppermute(last, axis, up)
        after = lax.ppermute(leading, axis, down)
        array = jnp.concatenate([before, array, after], axis=dim)
    return array


def shifted(value, axis, steps):
    count = lax.axis_size(axis)
    pairs = [(source, (source + steps) % count) for source in range(count)]
    return lax.ppermute(value, axis, pairs)


def place_tile(tile, offset_pos):
    return jnp.pad(tile, ((0, 0), (offset_pos, 2 - offset_pos), (0, 0)))


def shards(stiffness, block_cols, basis, patch_reach):
    blocks = stiffness.shape[0]
    block_size = stiffness.shape[2]
    row_count = basis.shape[0]
    groups = basis.shape[1]
    local_cols = basis.shape[2]
    slab_count = lax.axis_size("blk")
    slab_index = lax.axis_index("blk")
    total_blocks = blocks * slab_count
    reach_low = lax.dynamic_index_in_dim(patch_reach, (slab_index - 1) % slab_count, 0, False)
    reach_high = lax.dynamic_index_in_dim(patch_reach, (slab_index + 1) % slab_count, 0, False)
    block_row = jnp.arange(row_count, dtype=jnp.int32) // block_size
    lower_mask = block_row[:, None] < reach_low[None, :, 1]
    upper_mask = block_row[:, None] >= blocks - reach_high[None, :, 0]
    support = jnp.stack([lower_mask, jnp.ones_like(lower_mask), upper_mask], 1)
    masked = jnp.where(support, basis, jnp.zeros_like(basis))
    rim_width = 2 * block_size
    padded = extended_2(masked, (("blk", 0),), rim_width)
    zero_rim = jnp.zeros((rim_width, 1, local_cols), masked.dtype)
    lower_rim = jnp.concatenate([padded[:rim_width, 1:], zero_rim], 1)
    upper_rim = jnp.concatenate([zero_rim, padded[rim_width + row_count :, :2]], 1)
    extended = jnp.concatenate([lower_rim, masked, upper_rim], 0)
    extended = extended.reshape(blocks + 4, block_size, groups * local_cols)
    position = (block_cols - slab_index * blocks + 2) % total_blocks
    picked = jnp.take(extended, position, axis=0)
    stiff_image = jnp.einsum(
        "rsij,rsjc->ric", stiffness, picked, preferred_element_type=jnp.float32
    )
    stiff_image = stiff_image.astype(jnp.bfloat16).reshape(row_count, groups, local_cols)
    tile_sums = jnp.einsum(
        "rgl,rhc->glhc",
        masked,
        lax.all_gather(stiff_image, "col", axis=2, tiled=True),
        preferred_element_type=jnp.float32,
    )
    from_prev = shifted(tile_sums[2], "blk", 1)
    from_next = shifted(tile_sums[0], "blk", -1)
    return place_tile(from_prev, 0) + place_tile(tile_sums[1], 1) + place_tile(from_next, 2)


def solution(mesh):
    in_specs = (
        P("blk", None, None, None),
        P("blk", None),
        P("blk", None, "col"),
        P(None, "col", None),
    )
    out_specs = P(("blk", "col"), None, None)
    return jax.shard_map(shards, mesh=mesh, in_specs=in_specs, out_specs=out_specs, check_vma=False)
```

profile of v0, /device:TPU:1, one launch (start us, length us, event | category | flops | bytes accessed | tf_op | source)
XLA Modules:
  0.0 118.4 jit_solution(4530870687081001309)
XLA Ops:
  6.5 0.0 copy-start
  6.5 0.0 copy-start.1
  6.5 0.0 all-gather.2.cloned.1.call-start
  6.6 0.1 pad.21.clone
  6.6 0.7 dynamic-slice_bitcast_fusion.1
  7.3 0.2 broadcast_compare_fusion.1
  7.6 1.5 %add_select_fusion = bf16[1024,3,128]{2,0,1:T(8,128)(2,1)S(1)} fusion(bf16[1024,3,128]{2,0,1:T(8,128)(2,1)} %param.6, pred[1024,1,128]{2,0,1:T(8,128)(4,1)S(1)} %get-tuple-element.15, pred[1024,1,128]{2,0,1:T(8,128)(4,1)S(1)} %get-tuple-element.14, pred[3]{0:T(512)(128)(4,1)S(1)} %pad.21.clone), kind=kLoop, calls=%fused_computation.11 | loop fusion | flops 1179648 | bytes 1835011 | tf_op jit(solution)/shard_map/jit(_where)/select_n | solution.py:45
  9.1 2.7 %collective-permute-start = (bf16[256,3,128]{2,0,1:T(8,128)(2,1)S(1)}, bf16[256,3,128]{2,0,1:T(8,128)(2,1)S(1)}, u32[]{:S(2)}, u32[]{:S(2)}) collective-permute-start(bf16[256,3,128]{2,0,1:T(8,128)(2,1)S(1)} %get-tuple-element.10), channel_id=1, source_target_pairs={{0,4},{4,8},{8,12},{12,16},{16,20},{20,24},{24,28},{28,0},{1,5},{5... | collective-permute-start | bytes 589832 | tf_op jit(solution)/shard_map/ppermute | solution.py:14
  11.8 0.0 collective-permute-start.1
  11.8 0.0 copy-done.1
  11.8 0.1 copy.8
  11.9 0.1 copy.10
  12.0 0.1 reshape.126
  12.1 2.3 %collective-permute-done = bf16[256,3,128]{2,0,1:T(8,128)(2,1)S(1)} collective-permute-done((bf16[256,3,128]{2,0,1:T(8,128)(2,1)S(1)}, bf16[256,3,128]{2,0,1:T(8,128)(2,1)S(1)}, u32[]{:S(2)}, u32[]{:S(2)}) %collective-permute-start) | collective-permute-done | bytes 196640 | tf_op jit(solution)/shard_map/ppermute | solution.py:14
  14.4 4.0 %collective-permute-done.1 = bf16[256,3,128]{2,0,1:T(8,128)(2,1)S(1)} collective-permute-done((bf16[256,3,128]{2,0,1:T(8,128)(2,1)S(1)}, bf16[256,3,128]{2,0,1:T(8,128)(2,1)S(1)}, u32[]{:S(2)}, u32[]{:S(2)}) %collective-permute-start.1) | collective-permute-done | bytes 196640 | tf_op jit(solution)/shard_map/ppermute | solution.py:15
  18.4 0.1 fusion.12
  18.5 8.3 %copy.20 = bf16[1536,3,128]{2,1,0:T(4,128)(2,1)} copy(bf16[1536,3,128]{2,0,1:T(8,128)(2,1)S(1)} %fusion.12) | data formatting | bytes 2359296 | tf_op jit(solution)/shard_map/reshape | solution.py:52
  26.8 3.4 %reshape.137 = bf16[12,128,384]{2,1,0:T(8,128)(2,1)S(1)} reshape(bf16[1536,3,128]{2,1,0:T(4,128)(2,1)} %copy.20) | data formatting | bytes 2359296 | tf_op jit(solution)/shard_map/reshape | solution.py:52
  30.2 2.4 %gather_fusion = bf16[24,128,384]{2,1,0:T(8,128)(2,1)} fusion(bf16[12,128,384]{2,1,0:T(8,128)(2,1)S(1)} %reshape.137, s32[1024]{0:T(1024)S(1)} %pad_clamp_fusion), kind=kCustom, calls=%fused_computation | custom fusion | bytes 4718688 | tf_op jit(solution)/shard_map/jit(_take)/gather | solution.py:54
  32.6 4.3 %copy.12 = bf16[8,3,128,384]{2,3,1,0:T(8,128)(2,1)} copy(bf16[8,3,128,384]{3,2,1,0:T(8,128)(2,1)} %bitcast.34) | data formatting | bytes 4718592 | tf_op jit(solution)/shard_map/jit(_take)/gather | solution.py:54
  36.9 0.0 copy-done
  36.9 2.5 %fusion.9 = bf16[8,128,384]{1,2,0:T(8,128)(2,1)S(1)} fusion(bf16[8,3,128,128]{3,2,1,0:T(8,128)(2,1)S(1)} %copy-done, bf16[8,3,128,384]{2,3,1,0:T(8,128)(2,1)} %copy.12, pred[8,3]{1,0:T(8,128)(4,1)S(1)} %copy.8), kind=kOutput, calls=%fused_computation.13 | convolution fusion | flops 303562752 | bytes 3932184 | tf_op jit(solution)/shard_map/rsij,rsjc->ric/dot_general | solution.py:55
  39.4 0.5 copy.13
  39.9 0.3 reshape.123
  40.2 1.2 copy.14
  41.4 0.0 all-gather.2.cloned.1.call-update
  41.4 43.6 %all-gather.2.cloned.1.call-done = bf16[1024,3,512]{2,0,1:T(8,128)(2,1)} async-done(((bf16[1024,3,128]{2,0,1:T(8,128)(2,1)}), bf16[1024,3,512]{2,0,1:T(8,128)(2,1)}) %all-gather.2.cloned.1.call-update) | async-done | bytes 3145744 | tf_op jit(solution)/shard_map/all_gather | solution.py:62
  85.0 3.3 %fusion = f32[3,128,3,512]{3,1,2,0:T(8,128)S(1)} fusion(bf16[1024,3,512]{2,0,1:T(8,128)(2,1)} %all-gather.2.cloned.1.call-done, bf16[1024,3,128]{2,0,1:T(8,128)(2,1)S(1)} %add_select_fusion), kind=kOutput, calls=%fused_computation.1 | convolution fusion | flops 1207959552 | bytes 6291456 | tf_op jit(solution)/shard_map/rgl,rhc->glhc/dot_general | solution.py:59
  88.3 0.2 slice_bitcast_fusion.2
  88.6 1.8 %collective-permute-start.2 = (f32[128,3,512]{2,0,1:T(8,128)S(1)}, f32[128,3,512]{2,0,1:T(8,128)S(1)}, u32[]{:S(2)}, u32[]{:S(2)}) collective-permute-start(f32[128,3,512]{2,0,1:T(8,128)S(1)} %get-tuple-element.7), channel_id=1, source_target_pairs={{0,4},{4,8},{8,12},{12,16},{16,20},{20,24},{24,28},{28,0},{1,5},{5... | collective-permute-start | bytes 2359304 | tf_op jit(solution)/shard_map/ppermute | solution.py:23
  90.4 0.0 collective-permute-start.3
  90.4 14.7 %collective-permute-done.2 = f32[128,3,512]{2,0,1:T(8,128)S(1)} collective-permute-done((f32[128,3,512]{2,0,1:T(8,128)S(1)}, f32[128,3,512]{2,0,1:T(8,128)S(1)}, u32[]{:S(2)}, u32[]{:S(2)}) %collective-permute-start.2) | collective-permute-done | bytes 786464 | tf_op jit(solution)/shard_map/ppermute | solution.py:23
  105.0 5.2 %collective-permute-done.3 = f32[128,3,512]{2,0,1:T(8,128)S(1)} collective-permute-done((f32[128,3,512]{2,0,1:T(8,128)S(1)}, f32[128,3,512]{2,0,1:T(8,128)S(1)}, u32[]{:S(2)}, u32[]{:S(2)}) %collective-permute-start.3) | collective-permute-done | bytes 786464 | tf_op jit(solution)/shard_map/ppermute | solution.py:23
  110.2 1.3 %pad_add_fusion = f32[128,5,512]{2,0,1:T(8,128)} fusion(f32[128,3,512]{2,0,1:T(8,128)S(1)} %collective-permute-done.3, f32[128,3,512]{2,0,1:T(8,128)S(1)} %get-tuple-element.9, f32[128,3,512]{2,0,1:T(8,128)S(1)} %collective-permute-done.2), kind=kLoop, calls=%fused_computation.12 | loop fusion | flops 655360 | bytes 3670016 | tf_op jit(solution)/shard_map/add | solution.py:67
  (7 shorter events, 0.1 us)
Async XLA Ops:
  6.5 30.4 %copy-start = (bf16[8,3,128,128]{3,2,1,0:T(8,128)(2,1)S(1)}, bf16[8,3,128,128]{3,2,1,0:T(8,128)(2,1)}, u32[]{:S(2)}) copy-start(bf16[8,3,128,128]{3,2,1,0:T(8,128)(2,1)} %param.4) | copy-start | bytes 2359300
  6.5 5.3 %copy-start.1 = (s32[8,3]{0,1:T(4,128)S(1)}, s32[8,3]{0,1:T(4,128)}, u32[]{:S(2)}) copy-start(s32[8,3]{0,1:T(4,128)} %param.5) | copy-start | bytes 292
  6.5 78.5 %all-gather.2.cloned.1.call-start = ((), (), s32[]{:S(2)}) async-start(), calls=%async_computation | async-start | bytes 3932160 | tf_op jit(solution)/shard_map/all_gather | solution.py:62
  9.1 5.4 %collective-permute-start = (bf16[256,3,128]{2,0,1:T(8,128)(2,1)S(1)}, bf16[256,3,128]{2,0,1:T(8,128)(2,1)S(1)}, u32[]{:S(2)}, u32[]{:S(2)}) collective-permute-start(bf16[256,3,128]{2,0,1:T(8,128)(2,1)S(1)} %get-tuple-element.10), channel_id=1, source_target_pairs={{0,4},{4,8},{8,12},{12,16},{16,20},{20,24},{24,28},{28,0},{1,5},{5... | collective-permute-start | bytes 589832 | tf_op jit(solution)/shard_map/ppermute | solution.py:14
  11.8 6.6 %collective-permute-start.1 = (bf16[256,3,128]{2,0,1:T(8,128)(2,1)S(1)}, bf16[256,3,128]{2,0,1:T(8,128)(2,1)S(1)}, u32[]{:S(2)}, u32[]{:S(2)}) collective-permute-start(bf16[256,3,128]{2,0,1:T(8,128)(2,1)S(1)} %get-tuple-element.11), channel_id=1, source_target_pairs={{4,0},{8,4},{12,8},{16,12},{20,16},{24,20},{28,24},{0,28},{5,1},{9... | collective-permute-start | bytes 589832 | tf_op jit(solution)/shard_map/ppermute | solution.py:15
  88.6 16.5 %collective-permute-start.2 = (f32[128,3,512]{2,0,1:T(8,128)S(1)}, f32[128,3,512]{2,0,1:T(8,128)S(1)}, u32[]{:S(2)}, u32[]{:S(2)}) collective-permute-start(f32[128,3,512]{2,0,1:T(8,128)S(1)} %get-tuple-element.7), channel_id=1, source_target_pairs={{0,4},{4,8},{8,12},{12,16},{16,20},{20,24},{24,28},{28,0},{1,5},{5... | collective-permute-start | bytes 2359304 | tf_op jit(solution)/shard_map/ppermute | solution.py:23
  90.4 19.8 %collective-permute-start.3 = (f32[128,3,512]{2,0,1:T(8,128)S(1)}, f32[128,3,512]{2,0,1:T(8,128)S(1)}, u32[]{:S(2)}, u32[]{:S(2)}) collective-permute-start(f32[128,3,512]{2,0,1:T(8,128)S(1)} %get-tuple-element.8), channel_id=1, source_target_pairs={{0,28},{4,0},{8,4},{12,8},{16,12},{20,16},{24,20},{28,24},{1,29},{... | collective-permute-start | bytes 2359304 | tf_op jit(solution)/shard_map/ppermute | solution.py:23
Sparse Core Ops, SparseCore 0:
  41.5 43.4 all-gather.1
where the time goes:
time: 119 us; the launch traced here: 118 us
  waiting for transfers between devices  69.8 us (59%)
  local copies, waits for them, and re-layouts  21.6 us (18%)
  between operations  13.5 us (11%)
  matrix products  5.78 us (5%)
  starting transfers between devices  4.56 us (4%)
  other arithmetic  3.1 us (3%)
    all_gather x1, waiting for transfers between devices, shards(): lax.all_gather(stiff_image, 'col', axis=2, tiled=True)  43.6 us
    ppermute x2, waiting for transfers between devices, shifted(): return lax.ppermute(value, axis, pairs)  19.8 us
    reshape x2, local copies, waits for them, and re-layouts, shards(): extended = extended.reshape(blocks + 4, block_size, groups * local_cols)  11.6 us
    gather x2, local copies, waits for them, and re-layouts, shards(): picked = jnp.take(extended, position, axis=0)  6.73 us
    ppermute x1, waiting for transfers between devices, extended_2(): after = lax.ppermute(leading, axis, down)  4 us
    dot_general x1, matrix products, shards(): jnp.einsum('rgl,rhc->glhc', masked, lax.all_gather(stiff_image, 'col', ax...  3.29 us
    ppermute x1, starting transfers between devices, extended_2(): before = lax.ppermute(last, axis, up)  2.74 us
    dot_general x1, matrix products, shards(): jnp.einsum('rsij,rsjc->ric', stiffness, picked, preferred_element_type=jn...  2.48 us
  transfers between devices with their start and end apart: 5, of which 5 were waited for; matrix products, arithmetic and copies ran while one was open for 0% of the time, Pallas kernels for 0%

commit v1 on v0

--- a/solution.py
+++ b/solution.py
@@ -2,6 +2,12 @@
 import jax.numpy as jnp
 from jax import lax
 from jax.sharding import PartitionSpec as P
+
+
+def joined_along(parts, dim):
+    parts = jnp.moveaxis(parts, 0, dim)
+    shape = parts.shape
+    return parts.reshape(*shape[:dim], shape[dim] * shape[dim + 1], *shape[dim + 2 :])
 
 
 def extended_2(array, sides, width):
@@ -56,12 +62,26 @@
         "rsij,rsjc->ric", stiffness, picked, preferred_element_type=jnp.float32
     )
     stiff_image = stiff_image.astype(jnp.bfloat16).reshape(row_count, groups, local_cols)
-    tile_sums = jnp.einsum(
-        "rgl,rhc->glhc",
-        masked,
-        lax.all_gather(stiff_image, "col", axis=2, tiled=True),
-        preferred_element_type=jnp.float32,
-    )
+    length_2, position_2, rows = (lax.axis_size("col"), lax.axis_index("col"), stiff_image.shape[2])
+    upward = [(i_2, (i_2 + 1) % length_2) for i_2 in range(length_2)]
+    behind = [(i_2, (i_2 - 1) % length_2) for i_2 in range(length_2)]
+    half = length_2 // 2
+    parts = {}
+    from_left = from_right = stiff_image
+    for turn in range(half + 1):
+        next_left = lax.ppermute(from_left, "col", upward) if turn < half else None
+        next_right = lax.ppermute(from_right, "col", behind) if turn < length_2 - half - 1 else None
+        parts[-turn] = jnp.einsum(
+            "rgl,rhc->glhc", masked, from_left, preferred_element_type=jnp.float32
+        )
+        if 0 < turn < length_2 - half:
+            parts[turn] = jnp.einsum(
+                "rgl,rhc->glhc", masked, from_right, preferred_element_type=jnp.float32
+            )
+        from_left, from_right = (next_left, next_right)
+    parts = jnp.stack([parts[k] for k in sorted(parts)])
+    parts = parts[(jnp.arange(length_2) - position_2 + half) % length_2]
+    tile_sums = joined_along(parts, 3)
     from_prev = shifted(tile_sums[2], "blk", 1)
     from_next = shifted(tile_sums[0], "blk", -1)
     return place_tile(from_prev, 0) + place_tile(tile_sums[1], 1) + place_tile(from_next, 2)

time: 119 us -> 119 us (level)
  between operations: 13.5 us -> 0.15 us
  local copies, waits for them, and re-layouts: 21.6 us -> 29.5 us
  starting transfers between devices: 4.56 us -> 7.88 us
  waiting for transfers between devices: 69.8 us -> 71 us
    ppermute x0 -> x3, waiting for transfers between devices: none -> 46.8 us  [the longest x2 31.6 us: shards(): next_left = lax.ppermute(from_left, 'col', upward) if turn < half else None]
    all_gather x1 -> x0, waiting for transfers between devices: 43.6 us -> none  [shards(): lax.all_gather(stiff_image, 'col', axis=2, tiled=True)]
    slice x0 -> x4, local copies, waits for them, and re-layouts: none -> 4.37 us  [the longest x2 2.96 us: shards(): from_prev = shifted(tile_sums[2], 'blk', 1)]
    ppermute x0 -> x3, starting transfers between devices: none -> 3.53 us  [the longest x2 2.58 us: shards(): next_left = lax.ppermute(from_left, 'col', upward) if turn < half else None]
    gather x0 -> x1, local copies, waits for them, and re-layouts: none -> 2.13 us  [shards(): parts = parts[(jnp.arange(length_2) - position_2 + half) % length_2]]
    ppermute x2, waiting for transfers between devices: 19.8 us -> 17.9 us  [shifted(): return lax.ppermute(value, axis, pairs)]
    add x0 -> x1, local copies, waits for them, and re-layouts: none -> 1.46 us  [shards(): place_tile(from_prev, 0) + place_tile(tile_sums[1], 1)]
    dot_general x1 -> x4, matrix products: 3.29 us -> 3.51 us  [the longest x3 1.79 us: shards(): jnp.einsum('rgl,rhc->glhc', masked, from_left, preferred_element_type=jnp...]
  transfers between devices with their start and end apart: 5 -> 7, of which waited for: 5 -> 7; matrix products, arithmetic and copies ran while one was open for 0% -> 4% of each run, Pallas kernels for 0% -> 0%
where the time goes in v1:
time: 119 us; the launch traced here: 118 us
  waiting for transfers between devices  71 us (60%)
  local copies, waits for them, and re-layouts  29.5 us (25%)
  starting transfers between devices  7.88 us (7%)
  matrix products  5.99 us (5%)
  other arithmetic  3.55 us (3%)
    ppermute x2, waiting for transfers between devices, shards(): next_left = lax.ppermute(from_left, 'col', upward) if turn < half else None  31.6 us
    ppermute x2, waiting for transfers between devices, shifted(): return lax.ppermute(value, axis, pairs)  17.9 us
    ppermute x1, waiting for transfers between devices, shards(): lax.ppermute(from_right, 'col', behind)  15.2 us
    reshape x2, local copies, waits for them, and re-layouts, shards(): extended = extended.reshape(blocks + 4, block_size, groups * local_cols)  11.6 us
    gather x2, local copies, waits for them, and re-layouts, shards(): picked = jnp.take(extended, position, axis=0)  6.73 us
    ppermute x1, waiting for transfers between devices, extended_2(): after = lax.ppermute(leading, axis, down)  4 us
    slice x2, local copies, waits for them, and re-layouts, shards(): from_prev = shifted(tile_sums[2], 'blk', 1)  2.96 us
    ppermute x1, starting transfers between devices, extended_2(): before = lax.ppermute(last, axis, up)  2.74 us
  transfers between devices with their start and end apart: 7, of which 7 were waited for; matrix products, arithmetic and copies ran while one was open for 4% of the time, Pallas kernels for 0%

profile of v1, /device:TPU:1, one launch (start us, length us, event | category | flops | bytes accessed | tf_op | source)
XLA Modules:
  0.0 118.1 jit_solution(12272065260451694636)
XLA Ops:
  0.0 0.0 copy-start
  0.0 0.0 copy-start.1
  0.0 0.8 dynamic-slice_bitcast_fusion.1
  0.8 0.1 pad.25.clone
  0.9 0.2 broadcast_compare_fusion.1
  1.1 1.5 %add_select_fusion = bf16[1024,3,128]{2,0,1:T(8,128)(2,1)S(1)} fusion(bf16[1024,3,128]{2,0,1:T(8,128)(2,1)} %param.6, pred[1024,1,128]{2,0,1:T(8,128)(4,1)S(1)} %get-tuple-element.15, pred[1024,1,128]{2,0,1:T(8,128)(4,1)S(1)} %get-tuple-element.14, pred[3]{0:T(512)(128)(4,1)S(1)} %pad.25.clone), kind=kLoop, calls=%fused_computation.11 | loop fusion | flops 1179648 | bytes 1835011 | tf_op jit(solution)/shard_map/jit(_where)/select_n | solution.py:51
  2.6 2.7 %collective-permute-start = (bf16[256,3,128]{2,0,1:T(8,128)(2,1)S(1)}, bf16[256,3,128]{2,0,1:T(8,128)(2,1)S(1)}, u32[]{:S(2)}, u32[]{:S(2)}) collective-permute-start(bf16[256,3,128]{2,0,1:T(8,128)(2,1)S(1)} %get-tuple-element.10), channel_id=1, source_target_pairs={{0,4},{4,8},{8,12},{12,16},{16,20},{20,24},{24,28},{28,0},{1,5},{5... | collective-permute-start | bytes 589832 | tf_op jit(solution)/shard_map/ppermute | solution.py:20
  5.3 0.0 collective-permute-start.1
  5.3 0.0 copy-done.1
  5.4 0.1 copy.13
  5.4 0.1 reshape.185
  5.5 0.1 copy.11
  5.6 2.3 %collective-permute-done = bf16[256,3,128]{2,0,1:T(8,128)(2,1)S(1)} collective-permute-done((bf16[256,3,128]{2,0,1:T(8,128)(2,1)S(1)}, bf16[256,3,128]{2,0,1:T(8,128)(2,1)S(1)}, u32[]{:S(2)}, u32[]{:S(2)}) %collective-permute-start) | collective-permute-done | bytes 196640 | tf_op jit(solution)/shard_map/ppermute | solution.py:20
  8.0 4.0 %collective-permute-done.1 = bf16[256,3,128]{2,0,1:T(8,128)(2,1)S(1)} collective-permute-done((bf16[256,3,128]{2,0,1:T(8,128)(2,1)S(1)}, bf16[256,3,128]{2,0,1:T(8,128)(2,1)S(1)}, u32[]{:S(2)}, u32[]{:S(2)}) %collective-permute-start.1) | collective-permute-done | bytes 196640 | tf_op jit(solution)/shard_map/ppermute | solution.py:21
  12.0 0.1 fusion.10
  12.1 8.3 %copy.36 = bf16[1536,3,128]{2,1,0:T(4,128)(2,1)} copy(bf16[1536,3,128]{2,0,1:T(8,128)(2,1)S(1)} %fusion.10) | data formatting | bytes 2359296 | tf_op jit(solution)/shard_map/reshape | solution.py:58
  20.3 3.4 %reshape.210 = bf16[12,128,384]{2,1,0:T(8,128)(2,1)S(1)} reshape(bf16[1536,3,128]{2,1,0:T(4,128)(2,1)} %copy.36) | data formatting | bytes 2359296 | tf_op jit(solution)/shard_map/reshape | solution.py:58
  23.7 2.4 %gather_fusion = bf16[24,128,384]{2,1,0:T(8,128)(2,1)} fusion(bf16[12,128,384]{2,1,0:T(8,128)(2,1)S(1)} %reshape.210, s32[1024]{0:T(1024)S(1)} %pad_clamp_fusion.1), kind=kCustom, calls=%fused_computation | custom fusion | bytes 4718688 | tf_op jit(solution)/shard_map/jit(_take)/gather | solution.py:60
  26.1 4.3 %copy.15 = bf16[8,3,128,384]{2,3,1,0:T(8,128)(2,1)} copy(bf16[8,3,128,384]{3,2,1,0:T(8,128)(2,1)} %bitcast.61) | data formatting | bytes 4718592 | tf_op jit(solution)/shard_map/jit(_take)/gather | solution.py:60
  30.4 0.0 copy-done
  30.4 2.5 %fusion.7 = bf16[8,128,384]{1,2,0:T(8,128)(2,1)S(1)} fusion(bf16[8,3,128,128]{3,2,1,0:T(8,128)(2,1)S(1)} %copy-done, bf16[8,3,128,384]{2,3,1,0:T(8,128)(2,1)} %copy.15, pred[8,3]{1,0:T(8,128)(4,1)S(1)} %copy.11), kind=kOutput, calls=%fused_computation.13 | convolution fusion | flops 303562752 | bytes 3932184 | tf_op jit(solution)/shard_map/rsij,rsjc->ric/dot_general | solution.py:61
  32.9 0.5 copy.16
  33.4 0.3 reshape.182
  33.8 1.2 copy.17
  34.9 1.7 %collective-permute-start.2 = (bf16[1024,3,128]{2,0,1:T(8,128)(2,1)}, bf16[1024,3,128]{2,0,1:T(8,128)(2,1)S(1)}, u32[]{:S(2)}, u32[]{:S(2)}) collective-permute-start(bf16[1024,3,128]{2,0,1:T(8,128)(2,1)} %copy.17), channel_id=1, source_target_pairs={{0,1},{1,2},{2,3},{3,0},{4,5},{5,6},{6,7},{7,4},{8,9},{9,10},{10,1... | collective-permute-start | bytes 2359304 | tf_op jit(solution)/shard_map/ppermute | solution.py:72
  36.6 1.0 collective-permute-start.4
  37.6 18.0 %collective-permute-done.2 = bf16[1024,3,128]{2,0,1:T(8,128)(2,1)S(1)} collective-permute-done((bf16[1024,3,128]{2,0,1:T(8,128)(2,1)}, bf16[1024,3,128]{2,0,1:T(8,128)(2,1)S(1)}, u32[]{:S(2)}, u32[]{:S(2)}) %collective-permute-start.2) | collective-permute-done | bytes 786464 | tf_op jit(solution)/shard_map/ppermute | solution.py:72
  55.6 0.9 collective-permute-start.3
  56.5 0.6 convolution_bitcast_fusion.1
  57.1 0.6 convolution_bitcast_fusion.2
  57.7 15.2 %collective-permute-done.4 = bf16[1024,3,128]{2,0,1:T(8,128)(2,1)} collective-permute-done((bf16[1024,3,128]{2,0,1:T(8,128)(2,1)}, bf16[1024,3,128]{2,0,1:T(8,128)(2,1)}, u32[]{:S(2)}, u32[]{:S(2)}) %collective-permute-start.4) | collective-permute-done | bytes 786464 | tf_op jit(solution)/shard_map/ppermute | solution.py:73
  73.0 1.7 %convolution_bitcast_fusion = f32[1,3,128,3,128]{4,2,3,1,0:T(8,128)S(1)} fusion(bf16[1024,3,128]{2,0,1:T(8,128)(2,1)S(1)} %add_select_fusion, bf16[1024,3,128]{2,0,1:T(8,128)(2,1)} %collective-permute-done.4), kind=kOutput, calls=%fused_computation.14 | convolution fusion | flops 301989888 | bytes 2162688 | tf_op jit(solution)/shard_map/rgl,rhc->glhc/dot_general | solution.py:78
  74.7 13.6 %collective-permute-done.3 = bf16[1024,3,128]{2,0,1:T(8,128)(2,1)S(1)} collective-permute-done((bf16[1024,3,128]{2,0,1:T(8,128)(2,1)S(1)}, bf16[1024,3,128]{2,0,1:T(8,128)(2,1)S(1)}, u32[]{:S(2)}, u32[]{:S(2)}) %collective-permute-start.3) | collective-permute-done | bytes 786464 | tf_op jit(solution)/shard_map/ppermute | solution.py:72
  88.3 0.6 convolution_bitcast_fusion.3
  88.9 0.2 pad_maximum_fusion
  89.1 2.1 %gather_fusion.1 = f32[4,3,128,3,128]{4,2,3,1,0:T(8,128)} fusion(f32[4,3,128,3,128]{4,2,3,1,0:T(8,128)S(1)} %pad_maximum_fusion, s32[1024]{0:T(1024)S(1)} %pad_clamp_fusion), kind=kCustom, calls=%fused_computation.1 | custom fusion | bytes 4718608 | tf_op jit(solution)/shard_map/gather | solution.py:83
  91.2 1.8 %fusion.28 = (f32[1,128,3,4,128]{4,1,2,0,3:T(8,128)S(1)}, f32[1,128,3,4,128]{4,1,2,0,3:T(8,128)S(1)}, f32[1,128,3,4,128]{4,1,2,0,3:T(8,128)S(1)}) fusion(f32[3,128,3,4,128]{4,1,2,0,3:T(8,128)} %bitcast.60), kind=kLoop, calls=%fused_computation.57 | loop fusion | bytes 4718592 | tf_op jit(solution)/shard_map/slice | solution.py:85
  93.0 1.2 %copy.24 = f32[1,128,3,4,128]{1,4,3,2,0:T(8,128)} copy(f32[1,128,3,4,128]{4,1,2,0,3:T(8,128)S(1)} %get-tuple-element.7) | data formatting | bytes 1572864 | tf_op jit(solution)/shard_map/slice | solution.py:85
  94.2 1.6 %collective-permute-start.5 = (f32[128,3,512]{0,2,1:T(8,128)}, f32[128,3,512]{0,2,1:T(8,128)}, u32[]{:S(2)}, u32[]{:S(2)}) collective-permute-start(f32[128,3,512]{0,2,1:T(8,128)} %bitcast.63), channel_id=1, source_target_pairs={{0,4},{4,8},{8,12},{12,16},{16,20},{20,24},{24,28},{28,0},{1,5},{5... | collective-permute-start | bytes 2359304 | tf_op jit(solution)/shard_map/ppermute | solution.py:29
  95.8 1.1 copy.26
  97.0 0.0 collective-permute-start.6
  97.0 0.3 copy.25
  97.2 13.3 %collective-permute-done.5 = f32[128,3,512]{0,2,1:T(8,128)} collective-permute-done((f32[128,3,512]{0,2,1:T(8,128)}, f32[128,3,512]{0,2,1:T(8,128)}, u32[]{:S(2)}, u32[]{:S(2)}) %collective-permute-start.5) | collective-permute-done | bytes 786464 | tf_op jit(solution)/shard_map/ppermute | solution.py:29
  110.5 4.6 %collective-permute-done.6 = f32[128,3,512]{0,2,1:T(8,128)} collective-permute-done((f32[128,3,512]{0,2,1:T(8,128)}, f32[128,3,512]{0,2,1:T(8,128)}, u32[]{:S(2)}, u32[]{:S(2)}) %collective-permute-start.6) | collective-permute-done | bytes 786464 | tf_op jit(solution)/shard_map/ppermute | solution.py:29
  115.1 1.5 %pad_add_fusion = f32[128,5,512]{0,2,1:T(8,128)S(1)} fusion(f32[128,3,512]{0,2,1:T(8,128)} %collective-permute-done.6, f32[128,3,512]{0,2,1:T(8,128)S(1)} %bitcast.62, f32[128,3,512]{0,2,1:T(8,128)} %collective-permute-done.5), kind=kLoop, calls=%fused_computation.12 | loop fusion | flops 655360 | bytes 3670016 | tf_op jit(solution)/shard_map/add | solution.py:87
  116.6 1.5 %copy.27 = f32[128,5,512]{2,0,1:T(8,128)} copy(f32[128,5,512]{0,2,1:T(8,128)S(1)} %pad_add_fusion) | data formatting | bytes 2621440 | tf_op jit(solution)/shard_map/add | solution.py:87
  (9 shorter events, 0.1 us)
Async XLA Ops:
  0.0 30.4 %copy-start = (bf16[8,3,128,128]{3,2,1,0:T(8,128)(2,1)S(1)}, bf16[8,3,128,128]{3,2,1,0:T(8,128)(2,1)}, u32[]{:S(2)}) copy-start(bf16[8,3,128,128]{3,2,1,0:T(8,128)(2,1)} %param.4) | copy-start | bytes 2359300
  0.0 5.3 %copy-start.1 = (s32[8,3]{0,1:T(4,128)S(1)}, s32[8,3]{0,1:T(4,128)}, u32[]{:S(2)}) copy-start(s32[8,3]{0,1:T(4,128)} %param.5) | copy-start | bytes 292
  2.6 5.4 %collective-permute-start = (bf16[256,3,128]{2,0,1:T(8,128)(2,1)S(1)}, bf16[256,3,128]{2,0,1:T(8,128)(2,1)S(1)}, u32[]{:S(2)}, u32[]{:S(2)}) collective-permute-start(bf16[256,3,128]{2,0,1:T(8,128)(2,1)S(1)} %get-tuple-element.10), channel_id=1, source_target_pairs={{0,4},{4,8},{8,12},{12,16},{16,20},{20,24},{24,28},{28,0},{1,5},{5... | collective-permute-start | bytes 589832 | tf_op jit(solution)/shard_map/ppermute | solution.py:20
  5.3 6.6 %collective-permute-start.1 = (bf16[256,3,128]{2,0,1:T(8,128)(2,1)S(1)}, bf16[256,3,128]{2,0,1:T(8,128)(2,1)S(1)}, u32[]{:S(2)}, u32[]{:S(2)}) collective-permute-start(bf16[256,3,128]{2,0,1:T(8,128)(2,1)S(1)} %get-tuple-element.11), channel_id=1, source_target_pairs={{4,0},{8,4},{12,8},{16,12},{20,16},{24,20},{28,24},{0,28},{5,1},{9... | collective-permute-start | bytes 589832 | tf_op jit(solution)/shard_map/ppermute | solution.py:21
  34.9 20.7 %collective-permute-start.2 = (bf16[1024,3,128]{2,0,1:T(8,128)(2,1)}, bf16[1024,3,128]{2,0,1:T(8,128)(2,1)S(1)}, u32[]{:S(2)}, u32[]{:S(2)}) collective-permute-start(bf16[1024,3,128]{2,0,1:T(8,128)(2,1)} %copy.17), channel_id=1, source_target_pairs={{0,1},{1,2},{2,3},{3,0},{4,5},{5,6},{6,7},{7,4},{8,9},{9,10},{10,1... | collective-permute-start | bytes 2359304 | tf_op jit(solution)/shard_map/ppermute | solution.py:72
  36.6 36.3 %collective-permute-start.4 = (bf16[1024,3,128]{2,0,1:T(8,128)(2,1)}, bf16[1024,3,128]{2,0,1:T(8,128)(2,1)}, u32[]{:S(2)}, u32[]{:S(2)}) collective-permute-start(bf16[1024,3,128]{2,0,1:T(8,128)(2,1)} %copy.17), channel_id=1, source_target_pairs={{0,3},{1,0},{2,1},{3,2},{4,7},{5,4},{6,5},{7,6},{8,11},{9,8},{10,9... | collective-permute-start | bytes 2359304 | tf_op jit(solution)/shard_map/ppermute | solution.py:73
  55.6 32.7 %collective-permute-start.3 = (bf16[1024,3,128]{2,0,1:T(8,128)(2,1)S(1)}, bf16[1024,3,128]{2,0,1:T(8,128)(2,1)S(1)}, u32[]{:S(2)}, u32[]{:S(2)}) collective-permute-start(bf16[1024,3,128]{2,0,1:T(8,128)(2,1)S(1)} %collective-permute-done.2), channel_id=1, source_target_pairs={{0,1},{1,2},{2,3},{3,0},{4,5},{5,6},{6,7},{7,4},{8,9},{9,10},{10,1... | collective-permute-start | bytes 2359304 | tf_op jit(solution)/shard_map/ppermute | solution.py:72
  94.2 16.3 %collective-permute-start.5 = (f32[128,3,512]{0,2,1:T(8,128)}, f32[128,3,512]{0,2,1:T(8,128)}, u32[]{:S(2)}, u32[]{:S(2)}) collective-permute-start(f32[128,3,512]{0,2,1:T(8,128)} %bitcast.63), channel_id=1, source_target_pairs={{0,4},{4,8},{8,12},{12,16},{16,20},{20,24},{24,28},{28,0},{1,5},{5... | collective-permute-start | bytes 2359304 | tf_op jit(solution)/shard_map/ppermute | solution.py:29
  97.0 18.1 %collective-permute-start.6 = (f32[128,3,512]{0,2,1:T(8,128)}, f32[128,3,512]{0,2,1:T(8,128)}, u32[]{:S(2)}, u32[]{:S(2)}) collective-permute-start(f32[128,3,512]{0,2,1:T(8,128)} %bitcast.24), channel_id=1, source_target_pairs={{0,28},{4,0},{8,4},{12,8},{16,12},{20,16},{24,20},{28,24},{1,29},{... | collective-permute-start | bytes 2359304 | tf_op jit(solution)/shard_map/ppermute | solution.py:29
